TPU v7x, 32 devices: a whole 2x2x4 slice. The times are simulated.
32 devices in a mesh: depth: 8 (over z, y), rows: 4 (over x, core).
Axes of the slice: x: 2, y: 2, z: 4, core: 2. Of those that a mesh axis runs over, the one named last changes fastest.
Arguments:
- density: float32 [4, 256, 8192], P('rows', 'depth'), may hold values from 0.00078125 to 0.015625
- attenuation: float32 [4, 256, 8192], P('rows', 'depth'), may hold values from 0.00078125 to 0.015625
- measured: float32 [4, 4, 8192], P(None, 'rows'), may hold values from -3 to 3
- angle_ids: int32 [4], replicated, may hold values from 0 to 359
- sides: int32 [4], replicated, may hold values from 0 to 1, as said below
Outputs:
- grad_density: float32 [4, 256, 8192], P('rows', 'depth')
- grad_attenuation: float32 [4, 256, 8192], P('rows', 'depth')
Inputs may be any that keep to these rules, and one draw needn't show every extreme that they name: Half of the 4 views have sides 1.
All inputs are finite; a program needn't handle non-finite values.
Results may differ from a plain program's by a relative error of at most 0.0001.
Values sent between devices are 32-bit elements; how exact they have to be, the bound alone decides.
No kernel may reach another device: no remote copies, remote signals or barrier semaphores. Data moves between devices by JAX's collectives and lax.ppermute only.
A program may use at most 64 MiB of HBM per device.

v0:
```python
import jax
import jax.numpy as jnp
from jax import lax
from jax.sharding import PartitionSpec as P

ANGLES = 360


def entering(value, axis, join, neutral):
    count, mine = (lax.axis_size(axis), lax.axis_index(axis))
    pieces = lax.all_gather(value, axis)
    subtotal = jnp.full_like(value, 0) + jnp.asarray(neutral, value.dtype)

    def step(position, subtotal):
        longer = join(subtotal, pieces[position])
        return jnp.where(position < mine, longer, subtotal)

    return lax.fori_loop(0, count - 1, step, subtotal)


def with_halo(block, sides, width):
    for axis, dim in sides:
        count = lax.axis_size(axis)
        forward = [(i, i + 1) for i in range(count - 1)]
        backward = [(target, source) for source, target in forward]
        low = lax.ppermute(
            lax.slice_in_dim(block, block.shape[dim] - width, None, axis=dim), axis, forward
        )
        high = lax.ppermute(lax.slice_in_dim(block, 0, width, axis=dim), axis, backward)
        block = jnp.concatenate([low, block, high], axis=dim)
    return block


def tilt_angle(angle_ids):
    return 0.8 * jnp.sin(jnp.pi * (angle_ids.astype(jnp.float32) + 0.5) / ANGLES - jnp.pi / 2)


def shifted_pair(field):
    widths = [(0, 0)] * (field.ndim - 1)
    from_left = jnp.pad(field[..., :-1], widths + [(1, 0)])
    from_right = jnp.pad(field[..., 1:], widths + [(0, 1)])
    return (from_left, from_right)


def resample(field, tilting):
    from_left, from_right = shifted_pair(field)
    return (
        (1.0 - jnp.abs(tilting)) * field
        + jnp.maximum(tilting, 0.0) * from_left
        + jnp.maximum(-tilting, 0.0) * from_right
    )


def resample_back(field, tilting):
    from_left, from_right = shifted_pair(field)
    return (
        (1.0 - jnp.abs(tilting)) * field
        + jnp.maximum(tilting, 0.0) * from_right
        + jnp.maximum(-tilting, 0.0) * from_left
    )


def strict_cumsum(field):
    depth_cells = field.shape[2]
    row_ids = lax.broadcasted_iota(jnp.int32, (depth_cells, depth_cells), 0)
    col_ids = lax.broadcasted_iota(jnp.int32, (depth_cells, depth_cells), 1)
    strictly_lower = (row_ids > col_ids).astype(jnp.float32)
    return jnp.einsum("ij,vrjc->vric", strictly_lower, field, precision=lax.Precision.HIGHEST)


def combine_sum(earlier, later):
    return earlier + later


def prefix_total(slab_values):
    earlier = entering(slab_values, "depth", combine_sum, jnp.zeros_like(slab_values))
    overall = lax.psum(slab_values, "depth")
    return (earlier, overall)


def detector_blur(image):
    padded = with_halo(image, (("rows", 1),), 1)
    return 0.25 * padded[:, :-2] + 0.5 * padded[:, 1:-1] + 0.25 * padded[:, 2:]


def on_device(density, attenuation, measured, angle_ids, sides):
    grad_density = jnp.zeros(density.shape, jnp.float32)
    grad_attenuation = jnp.zeros(density.shape, jnp.float32)
    tilting = tilt_angle(angle_ids)[:, None, None, None]
    far_side = (sides == 1)[:, None, None, None]
    emission = resample(density[None], tilting)
    absorb = resample(attenuation[None], tilting)
    before_absorb = strict_cumsum(absorb)
    absorb_in, absorb_all = prefix_total(jnp.sum(absorb, axis=2))
    nearer_sum = absorb_in[:, :, None, :] + before_absorb
    depth_sum = jnp.where(far_side, absorb_all[:, :, None, :] - nearer_sum - absorb, nearer_sum)
    transmit = jnp.exp(-depth_sum)
    radiance = emission * transmit
    before_radiance = strict_cumsum(radiance)
    radiance_in, signal = prefix_total(jnp.sum(radiance, axis=2))
    residual = detector_blur(signal) - measured
    back_signal = detector_blur(residual)[:, :, None, :]
    emitted_before = radiance_in[:, :, None, :] + before_radiance
    behind = jnp.where(far_side, emitted_before, signal[:, :, None, :] - emitted_before - radiance)
    grad_density = grad_density + jnp.sum(resample_back(back_signal * transmit, tilting), axis=0)
    grad_attenuation = grad_attenuation + jnp.sum(
        resample_back(-back_signal * behind, tilting), axis=0
    )
    return (grad_density, grad_attenuation)


def solution(mesh):
    placed = (P("rows", "depth", None), P("rows", "depth", None), P(None, "rows", None), P(), P())
    return jax.shard_map(
        on_device,
        mesh=mesh,
        in_specs=placed,
        out_specs=(P("rows", "depth", None), P("rows", "depth", None)),
        check_vma=False,
    )
```

profile of v0, /device:TPU:1, one launch (start us, length us, event | category | flops | bytes accessed | tf_op | source)
XLA Modules:
  0.0 301.4 jit_solution(13441340693976916239)
XLA Ops:
  7.2 0.0 all-gather.7.cloned.1.call-start
  7.2 0.7 abs_subtract_fusion
  7.9 2.0 fusion.29
  9.9 0.3 pad_bitcast_fusion
  10.3 1.0 copy-done.3
  11.2 1.8 fusion.10
  13.0 1.6 fusion.28
  14.7 3.2 %pad_bitcast_fusion.2 = (f32[32,8192]{1,0:T(8,128)}, f32[32,8192]{1,0:T(8,128)}) fusion(f32[1,1,32,8191]{3,2,1,0:T(8,128)} %get-tuple-element.227, f32[1,1,32,8191]{3,2,1,0:T(8,128)} %get-tuple-element.226), kind=kLoop, calls=%fused_computation.36 | loop fusion | bytes 4194048 | tf_op jit(solution)/shard_map/mul | solution.py:50
  17.9 35.9 %all-gather.7.cloned.1.call-done = f32[8,4,8192]{2,1,0:T(4,128)} async-done(((f32[1,4,8192]{2,1,0:T(4,128)}), f32[8,4,8192]{2,1,0:T(4,128)}) %all-gather.7.cloned.1.call-update) | async-done | bytes 1048592 | tf_op jit(solution)/shard_map/all_gather | solution.py:11
  53.8 0.7 all-reduce.11.cloned.1.call-update
  54.6 0.0 all-gather.9.cloned.1.call-start
  54.6 8.0 %while.28 = (s32[]{:T(128)}, f32[4,1,8192]{2,1,0:T(1,128)S(1)}, s32[]{:T(128)}, f32[8,4,1,8192]{3,1,0,2:T(4,128)}, s32[]{:T(128)}, /*index=5*/s32[]{:T(128)}) while((s32[]{:T(128)}, f32[4,1,8192]{2,1,0:T(1,128)S(1)}, s32[]{:T(128)}, f32[8,4,1,8192]{3,1,0,2:T(4,128)}, s32[]{:T(128)}, /*index=5*/s32[]{:T(128)}) %tuple.91), condition=%wide.region_3.4_spmd.clone, body=%wide.region_2.3_spmd.clone.sunk | while | flops 98308 | bytes 655461 | solution.py:18
  54.6 0.9 constant_dynamic-slice_fusion.4
  55.5 0.2 broadcast_select_fusion.6
  55.8 0.9 constant_dynamic-slice_fusion.4
  56.7 0.2 broadcast_select_fusion.6
  56.9 0.9 constant_dynamic-slice_fusion.4
  57.8 0.2 broadcast_select_fusion.6
  58.1 0.9 constant_dynamic-slice_fusion.4
  59.0 0.2 broadcast_select_fusion.6
  59.2 0.9 constant_dynamic-slice_fusion.4
  60.1 0.2 broadcast_select_fusion.6
  60.4 0.9 constant_dynamic-slice_fusion.4
  61.3 0.2 broadcast_select_fusion.6
  61.5 0.9 constant_dynamic-slice_fusion.4
  62.4 0.2 broadcast_select_fusion.6
  62.7 0.1 copy.25
  62.7 64.2 %all-reduce.11.cloned.1.call-done = f32[4,8192]{1,0:T(4,128)} async-done(((f32[4,8192]{1,0:T(4,128)}), f32[4,8192]{1,0:T(4,128)}) %all-reduce.11.cloned.1.call-update) | async-done | bytes 131088 | tf_op jit(solution)/shard_map/psum | solution.py:77
  127.0 9.0 %fusion.24 = (f32[4,8192]{1,0:T(4,128)}, f32[4,1,32,8192]{3,2,0,1:T(8,128)}) fusion(f32[32,8192]{1,0:T(8,128)} %get-tuple-element.234, f32[4]{0:T(128)S(1)} %get-tuple-element.231, f32[32,8192]{1,0:T(8,128)} %get-tuple-element.235, f32[4]{0:T(128)S(1)} %get-tuple-element.230, f32[32,8192]{1,0:T(8,128)S(1)} %bitcast.82, f32[4]{0:T(128)S(1)} %get-tuple-element.220, ...), kind=kOutput, calls=%fused_computation.49 | convolution fusion | flops 425690112 | bytes 10879028 | tf_op jit(solution)/shard_map/ij,vrjc->vric/dot_general | solution.py:68
  136.0 39.7 %all-gather.9.cloned.1.call-done = f32[8,4,8192]{2,1,0:T(4,128)} async-done(((f32[1,4,8192]{2,1,0:T(4,128)}), f32[8,4,8192]{2,1,0:T(4,128)}) %all-gather.9.cloned.1.call-update) | async-done | bytes 1048592 | tf_op jit(solution)/shard_map/all_gather | solution.py:11
  175.7 0.6 all-reduce.13.cloned.1.call-update
  176.2 72.8 %all-reduce.13.cloned.1.call-done = f32[4,1,8192]{2,0,1:T(4,128)} async-done(((f32[4,1,8192]{2,0,1:T(4,128)}), f32[4,1,8192]{2,0,1:T(4,128)}) %all-reduce.13.cloned.1.call-update) | async-done | bytes 131088 | tf_op jit(solution)/shard_map/psum | solution.py:77
  249.1 4.4 %collective-permute-start.1 = (f32[4,1,8192]{2,0,1:T(4,128)}, f32[4,1,8192]{2,0,1:T(4,128)S(1)}, u32[]{:S(2)}, u32[]{:S(2)}) collective-permute-start(f32[4,1,8192]{2,0,1:T(4,128)} %all-reduce.13.cloned.1.call-done), channel_id=1, source_target_pairs={{1,0},{2,1},{3,2},{5,4},{6,5},{7,6},{9,8},{10,9},{11,10},{13,12},{... | collective-permute-start | bytes 393224 | tf_op jit(solution)/shard_map/ppermute | solution.py:29
  253.5 3.0 collective-permute-start
  256.5 0.9 collective-permute-done.1
  257.4 1.3 collective-permute-done
  258.8 1.0 copy_subtract_fusion
  259.8 1.9 collective-permute-start.3
  261.7 4.4 %collective-permute-start.2 = (f32[4,1,8192]{2,0,1:T(4,128)S(1)}, f32[4,1,8192]{2,0,1:T(4,128)S(1)}, u32[]{:S(2)}, u32[]{:S(2)}) collective-permute-start(f32[4,1,8192]{2,0,1:T(4,128)S(1)} %copy_subtract_fusion), channel_id=1, source_target_pairs={{0,1},{1,2},{2,3},{4,5},{5,6},{6,7},{8,9},{9,10},{10,11},{12,13},{... | collective-permute-start | bytes 393224 | tf_op jit(solution)/shard_map/ppermute | solution.py:26
  266.2 8.0 %while.29 = (s32[]{:T(128)}, f32[4,1,8192]{2,1,0:T(1,128)S(1)}, s32[]{:T(128)}, f32[8,4,1,8192]{3,1,0,2:T(4,128)}, s32[]{:T(128)}, /*index=5*/s32[]{:T(128)}) while((s32[]{:T(128)}, f32[4,1,8192]{2,1,0:T(1,128)S(1)}, s32[]{:T(128)}, f32[8,4,1,8192]{3,1,0,2:T(4,128)}, s32[]{:T(128)}, /*index=5*/s32[]{:T(128)}) %tuple.90), condition=%wide.region_8.9_spmd.clone, body=%wide.region_7.8_spmd.clone.sunk | while | flops 98308 | bytes 655461 | solution.py:18
  266.2 0.9 constant_dynamic-slice_fusion.5
  267.1 0.2 broadcast_select_fusion.7
  267.3 0.9 constant_dynamic-slice_fusion.5
  268.3 0.2 broadcast_select_fusion.7
  268.5 0.9 constant_dynamic-slice_fusion.5
  269.4 0.2 broadcast_select_fusion.7
  269.6 0.9 constant_dynamic-slice_fusion.5
  270.6 0.2 broadcast_select_fusion.7
  270.8 0.9 constant_dynamic-slice_fusion.5
  271.7 0.2 broadcast_select_fusion.7
  271.9 0.9 constant_dynamic-slice_fusion.5
  272.9 0.2 broadcast_select_fusion.7
  273.1 0.9 constant_dynamic-slice_fusion.5
  274.0 0.2 broadcast_select_fusion.7
  274.2 0.1 copy.24
  274.3 0.1 fusion.25
  274.4 2.6 broadcast_multiply_fusion
  277.1 1.5 fusion.26
  278.5 0.7 copy-done
  279.2 0.3 copy-done.4
  279.5 0.3 copy-done.5
  279.8 5.0 %select_multiply_fusion = f32[4,1,32,8192]{3,2,0,1:T(8,128)S(1)} fusion(f32[4,8192]{1,0:T(4,128)S(1)} %bitcast.91, f32[4,8192]{1,0:T(4,128)S(1)} %get-tuple-element.218, pred[4]{0:T(512)(128)(4,1)S(1)} %broadcast_compare_fusion, f32[4,8192]{1,0:T(4,128)S(1)} %bitcast.92, f32[4,1,32,8192]{3,2,0,1:T(8,128)S(1)} %copy-done, f32[32,8192]{1,0:T(8,128)S(1)} %copy-done.4, ...), kind=kOutput, calls=%fused_computation.16 | convolution fusion | flops 420480000 | bytes 11927604 | tf_op jit(solution)/shard_map/ij,vrjc->vric/dot_general | solution.py:68
  284.8 3.5 %fusion.27 = (f32[4,1,32,8191]{3,2,0,1:T(8,128)S(1)}, f32[4,1,32,8191]{3,2,0,1:T(8,128)}) fusion(f32[4,1,32,8192]{3,2,0,1:T(8,128)S(1)} %select_multiply_fusion), kind=kLoop, calls=%fused_computation.52 | loop fusion | bytes 16775168 | tf_op jit(solution)/shard_map/slice | solution.py:41
  288.3 6.5 %add_reduce_fusion = (f32[32,8192]{1,0:T(8,128)}, f32[32,8192]{1,0:T(8,128)}) fusion(f32[4,1,32,8191]{3,2,0,1:T(8,128)} %get-tuple-element.225, f32[4,1,32,8191]{3,2,0,1:T(8,128)S(1)} %get-tuple-element.224, f32[4,1,32,8192]{3,2,0,1:T(8,128)S(1)} %select_multiply_fusion, f32[4]{0:T(128)S(1)} %get-tuple-element.231, f32[4]{0:T(128)S(1)} %get-tuple-element.230, ...), kind=kLoop, calls=%fused_computation.15 | loop fusion | flops 13107200 | bytes 27392048 | tf_op jit(solution)/shard_map/reduce_sum | solution.py:106
  (24 shorter events, 0.1 us)
Async XLA Ops:
  7.2 46.7 %all-gather.7.cloned.1.call-start = ((), (), s32[]{:S(2)}) async-start(), calls=%async_computation.2 | async-start | bytes 1179648 | tf_op jit(solution)/shard_map/all_gather | solution.py:11
  7.9 3.3 %copy-start.1 = (f32[1,32,8192]{2,1,0:T(8,128)S(1)}, f32[1,32,8192]{2,1,0:T(8,128)}, u32[]{:S(2)}) copy-start(f32[1,32,8192]{2,1,0:T(8,128)} %param.10) | copy-start | bytes 3145732
  9.9 3.1 %copy-start.2 = (f32[1,32,8192]{2,1,0:T(8,128)S(1)}, f32[1,32,8192]{2,1,0:T(8,128)}, u32[]{:S(2)}) copy-start(f32[1,32,8192]{2,1,0:T(8,128)} %param.9) | copy-start | bytes 3145732
  10.3 1.0 copy-start.3
  10.3 4.4 %copy-start.8 = (s32[4]{0:T(128)S(1)}, s32[4]{0:T(128)}, u32[]{:S(2)}) copy-start(s32[4]{0:T(128)} %param.13) | copy-start | bytes 52
  53.8 73.1 %all-reduce.11.cloned.1.call-start = ((), (), s32[]{:S(2)}) async-start(), calls=%async_computation | async-start | bytes 262144 | tf_op jit(solution)/shard_map/psum | solution.py:77
  54.6 121.1 %all-gather.9.cloned.1.call-start = ((), (), s32[]{:S(2)}) async-start(), calls=%async_computation.3 | async-start | bytes 1179648 | tf_op jit(solution)/shard_map/all_gather | solution.py:11
  127.0 131.8 %copy-start.6 = (f32[4,1,8192]{2,1,0:T(1,128)S(1)}, f32[4,1,8192]{2,1,0:T(1,128)}, u32[]{:S(2)}) copy-start(f32[4,1,8192]{2,1,0:T(1,128)} %param.11) | copy-start | bytes 393220
  175.7 73.4 %all-reduce.13.cloned.1.call-start = ((), (), s32[]{:S(2)}) async-start(), calls=%async_computation.1 | async-start | bytes 262144 | tf_op jit(solution)/shard_map/psum | solution.py:77
  249.1 8.4 %collective-permute-start.1 = (f32[4,1,8192]{2,0,1:T(4,128)}, f32[4,1,8192]{2,0,1:T(4,128)S(1)}, u32[]{:S(2)}, u32[]{:S(2)}) collective-permute-start(f32[4,1,8192]{2,0,1:T(4,128)} %all-reduce.13.cloned.1.call-done), channel_id=1, source_target_pairs={{1,0},{2,1},{3,2},{5,4},{6,5},{7,6},{9,8},{10,9},{11,10},{13,12},{... | collective-permute-start | bytes 393224 | tf_op jit(solution)/shard_map/ppermute | solution.py:29
  253.5 5.2 %collective-permute-start = (f32[4,1,8192]{2,0,1:T(4,128)}, f32[4,1,8192]{2,0,1:T(4,128)S(1)}, u32[]{:S(2)}, u32[]{:S(2)}) collective-permute-start(f32[4,1,8192]{2,0,1:T(4,128)} %all-reduce.13.cloned.1.call-done), channel_id=1, source_target_pairs={{0,1},{1,2},{2,3},{4,5},{5,6},{6,7},{8,9},{9,10},{10,11},{12,13},{... | collective-permute-start | bytes 393224 | tf_op jit(solution)/shard_map/ppermute | solution.py:26
  259.8 14.5 %collective-permute-start.3 = (f32[4,1,8192]{2,0,1:T(4,128)S(1)}, f32[4,1,8192]{2,0,1:T(4,128)S(1)}, u32[]{:S(2)}, u32[]{:S(2)}) collective-permute-start(f32[4,1,8192]{2,0,1:T(4,128)S(1)} %copy_subtract_fusion), channel_id=1, source_target_pairs={{1,0},{2,1},{3,2},{5,4},{6,5},{7,6},{9,8},{10,9},{11,10},{13,12},{... | collective-permute-start | bytes 393224 | tf_op jit(solution)/shard_map/ppermute | solution.py:29
  261.7 12.6 %collective-permute-start.2 = (f32[4,1,8192]{2,0,1:T(4,128)S(1)}, f32[4,1,8192]{2,0,1:T(4,128)S(1)}, u32[]{:S(2)}, u32[]{:S(2)}) collective-permute-start(f32[4,1,8192]{2,0,1:T(4,128)S(1)} %copy_subtract_fusion), channel_id=1, source_target_pairs={{0,1},{1,2},{2,3},{4,5},{5,6},{6,7},{8,9},{9,10},{10,11},{12,13},{... | collective-permute-start | bytes 393224 | tf_op jit(solution)/shard_map/ppermute | solution.py:26
  277.0 2.2 copy-start
  277.0 2.5 copy-start.4
  277.1 2.8 copy-start.5
  277.1 2.8 copy-start.7
Sparse Core Ops, SparseCore 0:
  13.1 40.6 all-gather.6
  58.0 68.9 all-reduce.10
  136.1 39.5 all-gather.8
  180.1 68.9 all-reduce.12
where the time goes:
time: 302 us; the launch traced here: 301 us
  waiting for transfers between devices  216 us (72%)
  local copies, waits for them, and re-layouts  27.4 us (9%)
  other arithmetic  15.5 us (5%)
  matrix products  14 us (5%)
  between operations  14 us (5%)
  starting transfers between devices  13.9 us (5%)
    psum x2, waiting for transfers between devices, prefix_total(): overall = lax.psum(slab_values, 'depth')  137 us
    all_gather x2, waiting for transfers between devices, entering(): pieces = lax.all_gather(value, axis)  75.6 us
    dot_general x2, matrix products, strict_cumsum(): jnp.einsum('ij,vrjc->vric', strictly_lower, field, precision=lax.Precisio...  14 us
    dynamic_slice x14, local copies, waits for them, and re-layouts, step(): longer = join(subtotal, pieces[position])  12.8 us
    ppermute x2, starting transfers between devices, with_halo(): lax.ppermute(lax.slice_in_dim(block, block.shape[dim] - width, None, axis...  7.42 us
    reduce_sum x1, other arithmetic, on_device(): jnp.sum(resample_back(-back_signal * behind, tilting), axis=0)  6.54 us
    ppermute x2, starting transfers between devices, with_halo(): lax.ppermute(lax.slice_in_dim(block, 0, width, axis=dim), axis, backward)  6.35 us
  transfers between devices with their start and end apart: 8, of which 6 were waited for; matrix products, arithmetic and copies ran while one was open for 7% of the time, Pallas kernels for 0%

commit v1 on v0

--- a/solution.py
+++ b/solution.py
@@ -1,9 +1,17 @@
+import functools
 import jax
 import jax.numpy as jnp
 from jax import lax
 from jax.sharding import PartitionSpec as P
 
 ANGLES = 360
+
+
+def _arrange_series(raw, row_axis):
+    return jnp.sum(jax.lax.all_gather(raw, row_axis), axis=0)
+
+
+lift_units_in = functools.partial(_arrange_series, row_axis="depth")
 
 
 def entering(value, axis, join, neutral):
@@ -74,7 +82,7 @@
 
 def prefix_total(slab_values):
     earlier = entering(slab_values, "depth", combine_sum, jnp.zeros_like(slab_values))
-    overall = lax.psum(slab_values, "depth")
+    overall = lift_units_in(slab_values)
     return (earlier, overall)
 
 

time: 302 us -> 166 us (0.55)
  waiting for transfers between devices: 216 us -> 77 us
    psum x2 -> x0, waiting for transfers between devices: 137 us -> none  [prefix_total(): overall = lax.psum(slab_values, 'depth')]
  transfers between devices with their start and end apart: 8 -> 6, of which waited for: 6 -> 4; matrix products, arithmetic and copies ran while one was open for 7% -> 8% of each run, Pallas kernels for 0% -> 0%
where the time goes in v1:
time: 166 us; the launch traced here: 165 us
  waiting for transfers between devices  77 us (46%)
  local copies, waits for them, and re-layouts  27.6 us (17%)
  other arithmetic  17.9 us (11%)
  between operations  14.3 us (9%)
  matrix products  14 us (8%)
  starting transfers between devices  13.8 us (8%)
    all_gather x2, waiting for transfers between devices, _arrange_series(): return jnp.sum(jax.lax.all_gather(raw, row_axis), axis=0)  75 us
    dot_general x2, matrix products, strict_cumsum(): jnp.einsum('ij,vrjc->vric', strictly_lower, field, precision=lax.Precisio...  14 us
    dynamic_slice x14, local copies, waits for them, and re-layouts, step(): longer = join(subtotal, pieces[position])  12.8 us
    ppermute x2, starting transfers between devices, with_halo(): lax.ppermute(lax.slice_in_dim(block, block.shape[dim] - width, None, axis...  7.53 us
    reduce_sum x1, other arithmetic, on_device(): jnp.sum(resample_back(-back_signal * behind, tilting), axis=0)  6.54 us
    ppermute x2, starting transfers between devices, with_halo(): lax.ppermute(lax.slice_in_dim(block, 0, width, axis=dim), axis, backward)  6.2 us
    slice x2, local copies, waits for them, and re-layouts, shifted_pair(): from_right = jnp.pad(field[..., 1:], widths + [(0, 1)])  4.92 us
    slice x2, local copies, waits for them, and re-layouts, shifted_pair(): from_left = jnp.pad(field[..., :-1], widths + [(1, 0)])  3.62 us
  transfers between devices with their start and end apart: 6, of which 4 were waited for; matrix products, arithmetic and copies ran while one was open for 8% of the time, Pallas kernels for 0%

profile of v1, /device:TPU:1, one launch (start us, length us, event | category | flops | bytes accessed | tf_op | source)
XLA Modules:
  0.0 165.0 jit_solution(8506780430681044729)
XLA Ops:
  7.2 0.7 abs_subtract_fusion
  7.9 2.0 %fusion.33 = (f32[1,1,32,8191]{3,2,1,0:T(8,128)S(1)}, f32[1,1,32,8191]{3,2,1,0:T(8,128)S(1)}) fusion(f32[1,1,32,8192]{3,2,1,0:T(8,128)} %bitcast.76), kind=kLoop, calls=%fused_computation.61 | loop fusion | bytes 4193792 | tf_op jit(solution)/shard_map/slice | solution.py:48
  9.9 0.3 pad_bitcast_fusion
  10.3 1.0 copy-done.3
  11.3 1.8 %fusion.12 = f32[4,8192]{1,0:T(4,128)} fusion(f32[32,8192]{1,0:T(8,128)S(1)} %get-tuple-element.234, f32[32,8192]{1,0:T(8,128)S(1)} %get-tuple-element.235, f32[32,8192]{1,0:T(8,128)S(1)} %bitcast.77, f32[4]{0:T(128)S(1)} %get-tuple-element.229, f32[4]{0:T(128)S(1)} %get-tuple-element.228, f32[4]{0:T(128)S(1)} %get-tuple-element.218), kind=kLoop, calls=%fused_computation.25 | loop fusion | flops 6258688 | bytes 3276848 | tf_op jit(solution)/shard_map/reduce_sum | solution.py:102
  13.0 0.0 all-gather.9.cloned.1.call-start
  13.1 1.6 fusion.32
  14.8 3.2 %pad_bitcast_fusion.2 = (f32[32,8192]{1,0:T(8,128)}, f32[32,8192]{1,0:T(8,128)}) fusion(f32[1,1,32,8191]{3,2,1,0:T(8,128)} %get-tuple-element.225, f32[1,1,32,8191]{3,2,1,0:T(8,128)} %get-tuple-element.224), kind=kLoop, calls=%fused_computation.43 | loop fusion | bytes 4194048 | tf_op jit(solution)/shard_map/mul | solution.py:58
  17.9 35.9 %all-gather.7.cloned.1.call-done = f32[8,4,8192]{2,1,0:T(4,128)} async-done(((f32[1,4,8192]{2,1,0:T(4,128)}), f32[8,4,8192]{2,1,0:T(4,128)}) %all-gather.7.cloned.1.call-update) | async-done | bytes 1048592 | tf_op jit(solution)/shard_map/all_gather | solution.py:11
  53.8 8.0 %while.28 = (s32[]{:T(128)}, f32[4,1,8192]{2,1,0:T(1,128)S(1)}, s32[]{:T(128)}, f32[8,4,1,8192]{3,1,0,2:T(4,128)}, s32[]{:T(128)}, /*index=5*/s32[]{:T(128)}) while((s32[]{:T(128)}, f32[4,1,8192]{2,1,0:T(1,128)S(1)}, s32[]{:T(128)}, f32[8,4,1,8192]{3,1,0,2:T(4,128)}, s32[]{:T(128)}, /*index=5*/s32[]{:T(128)}) %tuple.86), condition=%wide.region_3.4_spmd.clone, body=%wide.region_2.3_spmd.clone.sunk | while | flops 98308 | bytes 655461 | solution.py:26
  53.8 0.9 constant_dynamic-slice_fusion.4
  54.8 0.2 broadcast_select_fusion.6
  55.0 0.9 constant_dynamic-slice_fusion.4
  55.9 0.2 broadcast_select_fusion.6
  56.1 0.9 constant_dynamic-slice_fusion.4
  57.0 0.2 broadcast_select_fusion.6
  57.3 0.9 constant_dynamic-slice_fusion.4
  58.2 0.2 broadcast_select_fusion.6
  58.4 0.9 constant_dynamic-slice_fusion.4
  59.3 0.2 broadcast_select_fusion.6
  59.6 0.9 constant_dynamic-slice_fusion.4
  60.5 0.2 broadcast_select_fusion.6
  60.7 0.9 constant_dynamic-slice_fusion.4
  61.6 0.2 broadcast_select_fusion.6
  61.9 0.1 copy.27
  62.0 1.4 reduce_sum.61
  63.4 9.0 %fusion.13 = (f32[4,8192]{1,0:T(4,128)}, f32[4,1,32,8192]{3,2,0,1:T(8,128)}) fusion(f32[32,8192]{1,0:T(8,128)} %get-tuple-element.232, f32[4]{0:T(128)S(1)} %get-tuple-element.229, f32[32,8192]{1,0:T(8,128)} %get-tuple-element.233, f32[4]{0:T(128)S(1)} %get-tuple-element.228, f32[32,8192]{1,0:T(8,128)S(1)} %bitcast.80, f32[4]{0:T(128)S(1)} %get-tuple-element.218, ...), kind=kOutput, calls=%fused_computation.27 | convolution fusion | flops 425690112 | bytes 10879028 | tf_op jit(solution)/shard_map/ij,vrjc->vric/dot_general | solution.py:76
  72.4 39.1 %all-gather.9.cloned.1.call-done = f32[8,4,8192]{2,1,0:T(4,128)} async-done(((f32[1,4,8192]{2,1,0:T(4,128)}), f32[8,4,8192]{2,1,0:T(4,128)}) %all-gather.9.cloned.1.call-update) | async-done | bytes 1048592 | tf_op jit(solution)/shard_map/all_gather | solution.py:11
  111.5 1.4 reduce_sum.63
  113.0 0.1 reduce_sum.64
  113.1 4.3 %collective-permute-start.1 = (f32[4,1,8192]{2,1,0:T(1,128)S(1)}, f32[4,1,8192]{2,1,0:T(1,128)S(1)}, u32[]{:S(2)}, u32[]{:S(2)}) collective-permute-start(f32[4,1,8192]{2,1,0:T(1,128)S(1)} %reduce_sum.64), channel_id=1, source_target_pairs={{1,0},{2,1},{3,2},{5,4},{6,5},{7,6},{9,8},{10,9},{11,10},{13,12},{... | collective-permute-start | bytes 393224 | tf_op jit(solution)/shard_map/ppermute | solution.py:37
  117.4 3.0 %collective-permute-start = (f32[4,1,8192]{2,1,0:T(1,128)S(1)}, f32[4,1,8192]{2,1,0:T(1,128)S(1)}, u32[]{:S(2)}, u32[]{:S(2)}) collective-permute-start(f32[4,1,8192]{2,1,0:T(1,128)S(1)} %reduce_sum.64), channel_id=1, source_target_pairs={{0,1},{1,2},{2,3},{4,5},{5,6},{6,7},{8,9},{9,10},{10,11},{12,13},{... | collective-permute-start | bytes 393224 | tf_op jit(solution)/shard_map/ppermute | solution.py:34
  120.4 0.7 collective-permute-done.1
  121.1 1.2 collective-permute-done
  122.3 0.3 add_subtract_fusion
  122.6 1.9 %collective-permute-start.3 = (f32[4,1,8192]{2,1,0:T(1,128)S(1)}, f32[4,1,8192]{2,1,0:T(1,128)S(1)}, u32[]{:S(2)}, u32[]{:S(2)}) collective-permute-start(f32[4,1,8192]{2,1,0:T(1,128)S(1)} %add_subtract_fusion), channel_id=1, source_target_pairs={{1,0},{2,1},{3,2},{5,4},{6,5},{7,6},{9,8},{10,9},{11,10},{13,12},{... | collective-permute-start | bytes 393224 | tf_op jit(solution)/shard_map/ppermute | solution.py:37
  124.5 4.5 %collective-permute-start.2 = (f32[4,1,8192]{2,1,0:T(1,128)S(1)}, f32[4,1,8192]{2,1,0:T(1,128)S(1)}, u32[]{:S(2)}, u32[]{:S(2)}) collective-permute-start(f32[4,1,8192]{2,1,0:T(1,128)S(1)} %add_subtract_fusion), channel_id=1, source_target_pairs={{0,1},{1,2},{2,3},{4,5},{5,6},{6,7},{8,9},{9,10},{10,11},{12,13},{... | collective-permute-start | bytes 393224 | tf_op jit(solution)/shard_map/ppermute | solution.py:34
  129.1 8.0 %while.29 = (s32[]{:T(128)}, f32[4,1,8192]{2,1,0:T(1,128)S(1)}, s32[]{:T(128)}, f32[8,4,1,8192]{3,1,0,2:T(4,128)}, s32[]{:T(128)}, /*index=5*/s32[]{:T(128)}) while((s32[]{:T(128)}, f32[4,1,8192]{2,1,0:T(1,128)S(1)}, s32[]{:T(128)}, f32[8,4,1,8192]{3,1,0,2:T(4,128)}, s32[]{:T(128)}, /*index=5*/s32[]{:T(128)}) %tuple.85), condition=%wide.region_8.9_spmd.clone, body=%wide.region_7.8_spmd.clone.sunk | while | flops 98308 | bytes 655461 | solution.py:26
  129.1 0.9 constant_dynamic-slice_fusion.5
  130.0 0.2 broadcast_select_fusion.7
  130.2 0.9 constant_dynamic-slice_fusion.5
  131.2 0.2 broadcast_select_fusion.7
  131.4 0.9 constant_dynamic-slice_fusion.5
  132.3 0.2 broadcast_select_fusion.7
  132.5 0.9 constant_dynamic-slice_fusion.5
  133.5 0.2 broadcast_select_fusion.7
  133.7 0.9 constant_dynamic-slice_fusion.5
  134.6 0.2 broadcast_select_fusion.7
  134.8 0.9 constant_dynamic-slice_fusion.5
  135.7 0.2 broadcast_select_fusion.7
  136.0 0.9 constant_dynamic-slice_fusion.5
  136.9 0.2 broadcast_select_fusion.7
  137.1 0.1 copy.25
  137.2 0.3 multiply_add_fusion.1
  137.5 0.1 fusion.29
  137.6 0.1 copy.26
  137.7 2.6 %broadcast_multiply_fusion = f32[4,1,32,8192]{3,2,0,1:T(8,128)S(1)} fusion(f32[4,1,32,8192]{3,2,0,1:T(8,128)} %get-tuple-element.231, f32[4,8192]{1,0:T(4,128)S(1)} %bitcast.85), kind=kLoop, calls=%fused_computation.28 | loop fusion | flops 1048576 | bytes 8519680 | tf_op jit(solution)/shard_map/mul | solution.py:113
  140.3 1.5 fusion.30
  141.8 0.7 copy-done
  142.5 0.3 copy-done.4
  142.8 0.3 copy-done.5
  143.1 5.0 %select_multiply_fusion = f32[4,1,32,8192]{3,2,0,1:T(8,128)S(1)} fusion(f32[4,1,32,8192]{3,2,0,1:T(8,128)S(1)} %copy-done, f32[4,8192]{1,0:T(4,128)S(1)} %reduce_sum.63, f32[4,8192]{1,0:T(4,128)S(1)} %bitcast.90, f32[4,8192]{1,0:T(4,128)S(1)} %fusion.29, f32[32,8192]{1,0:T(8,128)S(1)} %copy-done.4, f32[4]{0:T(128)S(1)} %get-tuple-element.229, ...), kind=kOutput, calls=%fused_computation.16 | convolution fusion | flops 420480000 | bytes 11927604 | tf_op jit(solution)/shard_map/ij,vrjc->vric/dot_general | solution.py:76
  148.1 3.5 %fusion.31 = (f32[4,1,32,8191]{3,2,0,1:T(8,128)S(1)}, f32[4,1,32,8191]{3,2,0,1:T(8,128)}) fusion(f32[4,1,32,8192]{3,2,0,1:T(8,128)S(1)} %select_multiply_fusion), kind=kLoop, calls=%fused_computation.59 | loop fusion | bytes 16775168 | tf_op jit(solution)/shard_map/slice | solution.py:49
  151.6 6.5 %add_reduce_fusion = (f32[32,8192]{1,0:T(8,128)}, f32[32,8192]{1,0:T(8,128)}) fusion(f32[4,1,32,8191]{3,2,0,1:T(8,128)} %get-tuple-element.223, f32[4,1,32,8191]{3,2,0,1:T(8,128)S(1)} %get-tuple-element.222, f32[4,1,32,8192]{3,2,0,1:T(8,128)S(1)} %select_multiply_fusion, f32[4]{0:T(128)S(1)} %get-tuple-element.229, f32[4]{0:T(128)S(1)} %get-tuple-element.228, ...), kind=kLoop, calls=%fused_computation.15 | loop fusion | flops 13107200 | bytes 27392048 | tf_op jit(solution)/shard_map/reduce_sum | solution.py:114
  (21 shorter events, 0.1 us)
Async XLA Ops:
  7.2 46.7 %all-gather.7.cloned.1.call-start = ((), (), s32[]{:S(2)}) async-start(), calls=%async_computation | async-start | bytes 1179648 | tf_op jit(solution)/shard_map/all_gather | solution.py:11
  7.9 3.3 %copy-start.1 = (f32[1,32,8192]{2,1,0:T(8,128)S(1)}, f32[1,32,8192]{2,1,0:T(8,128)}, u32[]{:S(2)}) copy-start(f32[1,32,8192]{2,1,0:T(8,128)} %param.10) | copy-start | bytes 3145732
  9.9 3.2 %copy-start.2 = (f32[1,32,8192]{2,1,0:T(8,128)S(1)}, f32[1,32,8192]{2,1,0:T(8,128)}, u32[]{:S(2)}) copy-start(f32[1,32,8192]{2,1,0:T(8,128)} %param.9) | copy-start | bytes 3145732
  10.3 1.0 copy-start.3
  10.3 4.5 %copy-start.7 = (s32[4]{0:T(128)S(1)}, s32[4]{0:T(128)}, u32[]{:S(2)}) copy-start(s32[4]{0:T(128)} %param.13) | copy-start | bytes 52
  13.0 98.5 %all-gather.9.cloned.1.call-start = ((), (), s32[]{:S(2)}) async-start(), calls=%async_computation.1 | async-start | bytes 1179648 | tf_op jit(solution)/shard_map/all_gather | solution.py:11
  63.4 58.9 %copy-start.6 = (f32[4,1,8192]{2,1,0:T(1,128)S(1)}, f32[4,1,8192]{2,1,0:T(1,128)}, u32[]{:S(2)}) copy-start(f32[4,1,8192]{2,1,0:T(1,128)} %param.11) | copy-start | bytes 393220
  113.1 8.0 %collective-permute-start.1 = (f32[4,1,8192]{2,1,0:T(1,128)S(1)}, f32[4,1,8192]{2,1,0:T(1,128)S(1)}, u32[]{:S(2)}, u32[]{:S(2)}) collective-permute-start(f32[4,1,8192]{2,1,0:T(1,128)S(1)} %reduce_sum.64), channel_id=1, source_target_pairs={{1,0},{2,1},{3,2},{5,4},{6,5},{7,6},{9,8},{10,9},{11,10},{13,12},{... | collective-permute-start | bytes 393224 | tf_op jit(solution)/shard_map/ppermute | solution.py:37
  117.4 4.9 %collective-permute-start = (f32[4,1,8192]{2,1,0:T(1,128)S(1)}, f32[4,1,8192]{2,1,0:T(1,128)S(1)}, u32[]{:S(2)}, u32[]{:S(2)}) collective-permute-start(f32[4,1,8192]{2,1,0:T(1,128)S(1)} %reduce_sum.64), channel_id=1, source_target_pairs={{0,1},{1,2},{2,3},{4,5},{5,6},{6,7},{8,9},{9,10},{10,11},{12,13},{... | collective-permute-start | bytes 393224 | tf_op jit(solution)/shard_map/ppermute | solution.py:34
  122.6 14.6 %collective-permute-start.3 = (f32[4,1,8192]{2,1,0:T(1,128)S(1)}, f32[4,1,8192]{2,1,0:T(1,128)S(1)}, u32[]{:S(2)}, u32[]{:S(2)}) collective-permute-start(f32[4,1,8192]{2,1,0:T(1,128)S(1)} %add_subtract_fusion), channel_id=1, source_target_pairs={{1,0},{2,1},{3,2},{5,4},{6,5},{7,6},{9,8},{10,9},{11,10},{13,12},{... | collective-permute-start | bytes 393224 | tf_op jit(solution)/shard_map/ppermute | solution.py:37
  124.5 12.7 %collective-permute-start.2 = (f32[4,1,8192]{2,1,0:T(1,128)S(1)}, f32[4,1,8192]{2,1,0:T(1,128)S(1)}, u32[]{:S(2)}, u32[]{:S(2)}) collective-permute-start(f32[4,1,8192]{2,1,0:T(1,128)S(1)} %add_subtract_fusion), channel_id=1, source_target_pairs={{0,1},{1,2},{2,3},{4,5},{5,6},{6,7},{8,9},{9,10},{10,11},{12,13},{... | collective-permute-start | bytes 393224 | tf_op jit(solution)/shard_map/ppermute | solution.py:34
  140.3 2.2 %copy-start = (f32[4,1,32,8192]{3,2,0,1:T(8,128)S(1)}, f32[4,1,32,8192]{3,2,0,1:T(8,128)}, u32[]{:S(2)}) copy-start(f32[4,1,32,8192]{3,2,0,1:T(8,128)} %get-tuple-element.231) | copy-start | bytes 12582916
  140.3 2.5 %copy-start.4 = (f32[32,8192]{1,0:T(8,128)S(1)}, f32[32,8192]{1,0:T(8,128)}, u32[]{:S(2)}) copy-start(f32[32,8192]{1,0:T(8,128)} %get-tuple-element.232) | copy-start | bytes 3145732
  140.3 2.8 %copy-start.5 = (f32[32,8192]{1,0:T(8,128)S(1)}, f32[32,8192]{1,0:T(8,128)}, u32[]{:S(2)}) copy-start(f32[32,8192]{1,0:T(8,128)} %get-tuple-element.233) | copy-start | bytes 3145732
Sparse Core Ops, SparseCore 0:
  13.2 40.6 all-gather.6
  72.5 38.9 all-gather.8
